TPU v7x, 32 devices: a whole 2x2x4 slice. The times are simulated.
32 devices in a mesh: group: 2 (over x), ctx: 8 (over z, y), exp: 2 (over core).
Axes of the slice: x: 2, y: 2, z: 4, core: 2. Of those that a mesh axis runs over, the one named last changes fastest.
Arguments:
- prompt_query: bfloat16 [2, 2, 2048, 2048], P('group', 'exp', 'ctx'), may hold values from -6 to 6
- prompt_keys: bfloat16 [2, 2, 2048, 256], P('group', 'exp', 'ctx'), may hold values from -6 to 6
- prompt_values: bfloat16 [2, 2, 2048, 256], P('group', 'exp', 'ctx'), may hold values from -24 to 24
- lengths: int32 [2, 2], P(None, 'exp'), may hold values from 1025 to 2048
- decode_query: bfloat16 [2, 2, 128, 2048], P('group', 'exp', None, 'ctx'), may hold values from -6 to 6
- fresh_keys: bfloat16 [2, 2, 128, 256], P('group', 'exp'), may hold values from -6 to 6
- fresh_values: bfloat16 [2, 2, 128, 256], P('group', 'exp'), may hold values from -24 to 24
- x_dec: bfloat16 [2, 2, 128, 2048], P('group', 'exp', 'ctx'), may hold values from -0.59765625 to 0.59765625
- w_out: bfloat16 [2048, 2048], P('ctx'), may hold values from -0.125 to 0.125
- norm_gain: bfloat16 [2048], replicated, may hold values from 0.5 to 1.5
- w_gate_up: bfloat16 [16, 2048, 1536], P(('ctx', 'exp')), may hold values from -0.125 to 0.125
- w_down: bfloat16 [16, 768, 2048], P(('ctx', 'exp')), may hold values from -0.21875 to 0.21875
- expert_ids: int32 [2, 2, 128, 8], P('group', 'exp', 'ctx'), may hold values from 0 to 15, all different within a row; in each aligned block of 16 rows (0 to 15, 16 to 31, ..., all dimensions but the last counted through in order) at most 16 rows name the same one
- gate_weights: float32 [2, 2, 128, 8], P('group', 'exp', 'ctx'), may hold values from 0.1 to 1
Outputs:
- prompt_attention: bfloat16 [2, 2, 2048, 2048], P('group', 'exp', 'ctx')
- out_dec: bfloat16 [2, 2, 128, 2048], P('group', 'exp', 'ctx')
Inputs may be any that keep to these rules, and one draw needn't show every extreme that they name: `expert_ids`: the 8 experts of a row differ; among the rows of one device no expert is named more than 16 times.
All inputs are finite; a program needn't handle non-finite values.
Results may differ from a plain program's by a relative error of at most 0.025.
Values may be sent and summed in bfloat16 or wider, within the bound.
A program may use at most 128 MiB of HBM per device.

v0:
```python
import math
import jax
import jax.numpy as jnp
from jax import lax
from jax.sharding import PartitionSpec as P

HEAD_SIZE = 128
QUERY_HEADS = 16
KEY_VALUE_HEADS = 2
NEGATIVE_LIMIT = -1e30
EPSILON = 1e-06


def from_partner(block, axis, apart):
    count = lax.axis_size(axis)
    route = []
    for low in range(count):
        high = low | 1 << apart
        if high != low and high < count:
            route += [(low, high), (high, low)]
    return lax.ppermute(block, axis, route)


def blockwise(update, carried, key_row_list, value_row_list, positions, usable):
    row_count = key_row_list.shape[0]
    stride = math.gcd(row_count, 512)
    splits = row_count // stride

    def advance(status, members):
        return (update(status, *members), None)

    shaped = (
        key_row_list.reshape(splits, stride, key_row_list.shape[1]),
        value_row_list.reshape(splits, stride, value_row_list.shape[1]),
        positions.reshape(splits, stride),
        usable.reshape(splits, stride),
    )
    carried, unused_out = lax.scan(advance, carried, shaped)
    return carried


def body(
    prompt_query,
    prompt_keys,
    prompt_values,
    lengths,
    decode_query,
    fresh_keys,
    fresh_values,
    x_dec,
    w_out,
    norm_gain,
    w_gate_up,
    w_down,
    expert_ids,
    gate_weights,
):
    group_width = QUERY_HEADS // KEY_VALUE_HEADS
    scaling = HEAD_SIZE ** (-0.5)
    my_group = lax.axis_index("group")
    ctx_index = lax.axis_index("ctx")
    ctx_count = lax.axis_size("ctx")
    length_list = lengths[:, 0]
    length_mine = lax.dynamic_index_in_dim(length_list, my_group, keepdims=False)
    length_other = lax.dynamic_index_in_dim(length_list, 1 - my_group, keepdims=False)
    token_rows = prompt_query.shape[2]
    prompt_len = token_rows * ctx_count
    query_tensor = prompt_query[0, 0].reshape(token_rows, KEY_VALUE_HEADS, group_width, HEAD_SIZE)
    query_pos = ctx_index * token_rows + lax.iota(jnp.int32, token_rows)
    query_limit = jnp.minimum(length_mine, ctx_index * token_rows + token_rows)
    local_heads = decode_query.shape[3] // HEAD_SIZE
    samples = decode_query.shape[2]
    dec_queries = decode_query[0, 0].reshape(samples, local_heads, HEAD_SIZE)
    kv_head = ctx_index * local_heads // group_width

    def prefill_step(status, key_row_list, value_row_list, positions, usable):
        usable = usable & (positions < query_limit)

        def prefill_compute(carried):
            run_max, run_sum, weighted = carried
            key_parts = key_row_list.reshape(-1, KEY_VALUE_HEADS, HEAD_SIZE)
            value_parts = value_row_list.reshape(-1, KEY_VALUE_HEADS, HEAD_SIZE)
            scores = (
                jnp.einsum(
                    "qhgd,khd->hgqk", query_tensor, key_parts, preferred_element_type=jnp.float32
                )
                * scaling
            )
            keep_mask = usable[None, :] & (positions[None, :] <= query_pos[:, None])
            scores = jnp.where(keep_mask[None, None], scores, NEGATIVE_LIMIT)
            new_max = jnp.maximum(run_max, scores.max(-1))
            rescale = jnp.exp(run_max - new_max)
            weights = jnp.where(keep_mask[None, None], jnp.exp(scores - new_max[..., None]), 0.0)
            run_sum = rescale * run_sum + weights.sum(-1)
            weighted = rescale[..., None] * weighted + jnp.einsum(
                "hgqk,khd->hgqd",
                weights.astype(jnp.bfloat16),
                value_parts,
                preferred_element_type=jnp.float32,
            )
            return (new_max, run_sum, weighted)

        return lax.cond(jnp.any(usable), prefill_compute, lambda carried: carried, status)

    def make_decode():

        def decode_step(status, key_row_list, value_row_list, positions, usable):
            usable = usable & (positions < length_other)

            def decode_compute(carried):
                run_max, run_sum, weighted = carried
                scores = (
                    jnp.einsum(
                        "shd,kd->hsk", dec_queries, key_row_list, preferred_element_type=jnp.float32
                    )
                    * scaling
                )
                scores = jnp.where(usable[None, None], scores, NEGATIVE_LIMIT)
                new_max = jnp.maximum(run_max, scores.max(-1))
                rescale = jnp.exp(run_max - new_max)
                weights = jnp.where(usable[None, None], jnp.exp(scores - new_max[..., None]), 0.0)
                run_sum = rescale * run_sum + weights.sum(-1)
                weighted = rescale[..., None] * weighted + jnp.einsum(
                    "hsk,kd->hsd",
                    weights.astype(jnp.bfloat16),
                    value_row_list,
                    preferred_element_type=jnp.float32,
                )
                return (new_max, run_sum, weighted)

            return lax.cond(jnp.any(usable), decode_compute, lambda carried: carried, status)

        return decode_step

    decode_step = make_decode()
    pre_init = (
        jnp.full((KEY_VALUE_HEADS, group_width, token_rows), NEGATIVE_LIMIT, jnp.float32),
        jnp.zeros((KEY_VALUE_HEADS, group_width, token_rows), jnp.float32),
        jnp.zeros((KEY_VALUE_HEADS, group_width, token_rows, HEAD_SIZE), jnp.float32),
    )
    dec_init = (
        jnp.full((local_heads, samples), NEGATIVE_LIMIT, jnp.float32),
        jnp.zeros((local_heads, samples), jnp.float32),
        jnp.zeros((local_heads, samples, HEAD_SIZE), jnp.float32),
    )
    far_keys, far_values = from_partner((prompt_keys, prompt_values), "group", 0)
    peer_heads = lax.iota(jnp.int32, ctx_count) * local_heads // group_width
    key_chosen = jnp.take(
        far_keys[0, 0].reshape(token_rows, KEY_VALUE_HEADS, HEAD_SIZE), peer_heads, axis=1
    )
    value_chosen = jnp.take(
        far_values[0, 0].reshape(token_rows, KEY_VALUE_HEADS, HEAD_SIZE), peer_heads, axis=1
    )
    head_keys, head_values = (
        lax.all_to_all(key_chosen, "ctx", split_axis=1, concat_axis=0, tiled=True),
        lax.all_to_all(value_chosen, "ctx", split_axis=1, concat_axis=0, tiled=True),
    )
    key_piece = lax.all_gather(prompt_keys, "ctx", axis=2, tiled=True)
    value_piece = lax.all_gather(prompt_values, "ctx", axis=2, tiled=True)
    row_count = key_piece.shape[2]
    positions = lax.iota(jnp.int32, row_count)
    pre_state = blockwise(
        prefill_step, pre_init, key_piece[0, 0], value_piece[0, 0], positions, positions >= 0
    )
    all_positions = lax.iota(jnp.int32, prompt_len)
    dec_state = blockwise(
        make_decode(),
        dec_init,
        head_keys.reshape(prompt_len, HEAD_SIZE),
        head_values.reshape(prompt_len, HEAD_SIZE),
        all_positions,
        all_positions >= 0,
    )
    pre_max, pre_sum, pre_weighted = pre_state
    prompt_attn = pre_weighted / jnp.where(pre_sum > 0, pre_sum, 1.0)[..., None]
    prompt_attn = jnp.transpose(prompt_attn, (2, 0, 1, 3)).reshape(
        token_rows, QUERY_HEADS * HEAD_SIZE
    )
    prompt_attn = jnp.where((query_pos < length_mine)[:, None], prompt_attn, 0.0).astype(
        jnp.bfloat16
    )
    prompt_attention = prompt_attn.reshape(1, 1, token_rows, QUERY_HEADS * HEAD_SIZE)
    dec_max, dec_sum, dec_weighted = dec_state
    own_keys = lax.dynamic_slice_in_dim(fresh_keys[0, 0], kv_head * HEAD_SIZE, HEAD_SIZE, 1)
    own_values = lax.dynamic_slice_in_dim(fresh_values[0, 0], kv_head * HEAD_SIZE, HEAD_SIZE, 1)
    own_score = (
        jnp.einsum("shd,sd->hs", dec_queries, own_keys, preferred_element_type=jnp.float32)
        * scaling
    )
    final_max = jnp.maximum(dec_max, own_score)
    rescale = jnp.exp(dec_max - final_max)
    own_weight = jnp.exp(own_score - final_max)
    dec_sum = rescale * dec_sum + own_weight
    dec_weighted = (
        rescale[..., None] * dec_weighted
        + own_weight.astype(jnp.bfloat16).astype(jnp.float32)[..., None]
        * own_values.astype(jnp.float32)[None]
    )
    dec_attn = (dec_weighted / dec_sum[..., None]).astype(jnp.bfloat16)
    dec_attn = jnp.transpose(dec_attn, (1, 0, 2)).reshape(samples, local_heads * HEAD_SIZE)
    row_count = x_dec.shape[2]
    projected = lax.psum_scatter(
        jnp.dot(dec_attn, w_out, preferred_element_type=jnp.float32).astype(jnp.bfloat16),
        "ctx",
        scatter_dimension=0,
        tiled=True,
    ).astype(jnp.float32)
    residual = x_dec[0, 0].astype(jnp.float32) + projected
    normed = (
        residual
        * lax.rsqrt(jnp.mean(residual * residual, -1, keepdims=True) + EPSILON)
        * norm_gain.astype(jnp.float32)
    ).astype(jnp.bfloat16)
    model_width = normed.shape[1]
    top_count = expert_ids.shape[3]
    n_ctx = lax.axis_size("ctx")
    n_exp = lax.axis_size("exp")
    experts_all = w_gate_up.shape[0] * n_ctx * n_exp
    capacity = max(2, 2 * row_count * top_count // experts_all)
    flat_ids = expert_ids[0, 0].reshape(-1)
    one_hot = (flat_ids[:, None] == lax.iota(jnp.int32, experts_all)[None, :]).astype(jnp.int32)
    earlier = jnp.cumsum(one_hot, 0) - one_hot
    slot_rank = jnp.sum(earlier * one_hot, 1)
    target = flat_ids * capacity + slot_rank
    placing = (
        lax.iota(jnp.int32, experts_all * capacity)[:, None, None]
        == target.reshape(row_count, top_count)[None]
    ).any(-1)
    buffer = jnp.dot(
        placing.astype(jnp.bfloat16), normed, preferred_element_type=jnp.float32
    ).astype(jnp.bfloat16)
    buffer = buffer.reshape(experts_all, capacity, model_width)
    arrived = lax.all_to_all(buffer, ("ctx", "exp"), split_axis=0, concat_axis=0, tiled=True)
    flat_rows = arrived.reshape(-1, model_width)
    mixed = jnp.dot(flat_rows, w_gate_up[0], preferred_element_type=jnp.float32)
    hidden_units = mixed.shape[1] // 2
    hidden = (jax.nn.silu(mixed[:, :hidden_units]) * mixed[:, hidden_units:]).astype(jnp.bfloat16)
    produced = jnp.dot(hidden, w_down[0], preferred_element_type=jnp.float32).astype(jnp.bfloat16)
    outputs = produced.reshape(arrived.shape)
    returned = lax.all_to_all(outputs, ("ctx", "exp"), split_axis=0, concat_axis=0, tiled=True)
    picked = returned.reshape(experts_all * capacity, model_width)[target]
    gate_values = gate_weights[0, 0]
    moe = jnp.sum(
        picked.reshape(row_count, top_count, model_width).astype(jnp.float32)
        * gate_values[..., None],
        1,
    )
    out_dec = (residual + moe).astype(jnp.bfloat16).reshape(1, 1, row_count, model_width)
    return (prompt_attention, out_dec)


def solution(mesh):
    in_specs = (
        P("group", "exp", "ctx", None),
        P("group", "exp", "ctx", None),
        P("group", "exp", "ctx", None),
        P(None, "exp"),
        P("group", "exp", None, "ctx"),
        P("group", "exp", None, None),
        P("group", "exp", None, None),
        P("group", "exp", "ctx", None),
        P("ctx", None),
        P(),
        P(("ctx", "exp"), None, None),
        P(("ctx", "exp"), None, None),
        P("group", "exp", "ctx", None),
        P("group", "exp", "ctx", None),
    )
    out_specs = (P("group", "exp", "ctx", None), P("group", "exp", "ctx", None))
    return jax.shard_map(body, mesh=mesh, in_specs=in_specs, out_specs=out_specs, check_vma=False)
```

profile of v0, /device:TPU:25, one launch (start us, length us, event | category | flops | bytes accessed | tf_op | source)
XLA Modules:
  0.0 324.3 jit_solution(11437767902272269892)
XLA Ops:
  22.6 16.7 %all_to_all.40 = bf16[256,8,128]{2,0,1:T(8,128)(2,1)} all-to-all(bf16[256,8,128]{2,0,1:T(8,128)(2,1)S(1)} %get-tuple-element.486), channel_id=1, replica_groups=mesh['group'=2,'ctx'=8,'exp'=2] {'ctx'}, dimensions={1} | all-to-all | bytes 1048576 | tf_op jit(solution)/shard_map/all_to_all | solution.py:155
  39.3 6.3 %all-to-all-start.1 = ((bf16[256,8,128]{2,0,1:T(8,128)(2,1)}), bf16[256,8,128]{2,0,1:T(8,128)(2,1)}, u32[]{:S(2)}, u32[]{:S(2)}) async-start(bf16[256,8,128]{2,0,1:T(8,128)(2,1)} %get-tuple-element.485), calls=%async_computation.1 | async-start | bytes 1048576 | tf_op jit(solution)/shard_map/all_to_all | solution.py:156
  48.9 8.3 %all-to-all-done.1 = bf16[256,8,128]{2,0,1:T(8,128)(2,1)} async-done(((bf16[256,8,128]{2,0,1:T(8,128)(2,1)}), bf16[256,8,128]{2,0,1:T(8,128)(2,1)}, u32[]{:S(2)}, u32[]{:S(2)}) %all-to-all-start.1) | async-done | bytes 524320 | tf_op jit(solution)/shard_map/all_to_all | solution.py:156
  57.3 16.7 %while.31 = (s32[]{:T(128)}, f32[2,128]{1,0:T(2,128)S(1)}, f32[2,128]{1,0:T(2,128)S(1)}, f32[2,128,128]{2,1,0:T(8,128)S(1)}, s32[4,512]{1,0:T(4,128)S(1)}, /*ind...) while((s32[]{:T(128)}, f32[2,128]{1,0:T(2,128)S(1)}, ...), condition=%wide.region_13.15_spmd, body=%wide.region_7.14_spmd.sunk | while | flops 68355584 | bytes 2185460 | solution.py:38
  59.4 2.7 conditional.5
  64.2 2.7 conditional.5
  69.1 2.7 conditional.5
  81.0 61.8 %reduce-scatter.2.cloned.1.call-done = bf16[16,2048]{1,0:T(8,128)(2,1)} async-done(((bf16[128,2048]{1,0:T(8,128)(2,1)}), bf16[16,2048]{1,0:T(8,128)(2,1)}) %reduce-scatter.2.cloned.1.call-update) | async-done | bytes 65552 | tf_op jit(solution)/shard_map/reduce_scatter | solution.py:202
  146.1 7.9 %all-to-all-start.2 = ((bf16[16,16,2048]{2,1,0:T(8,128)(2,1)}), bf16[16,16,2048]{2,1,0:T(8,128)(2,1)}, u32[]{:S(2)}, u32[]{:S(2)}) async-start(bf16[16,16,2048]{2,1,0:T(8,128)(2,1)} %bitcast.131), calls=%async_computation.3 | async-start | bytes 2097152 | tf_op jit(solution)/shard_map/all_to_all | solution.py:233
  160.8 33.7 %all-gather.3.cloned.1.call-done = bf16[1,1,2048,256]{3,2,1,0:T(8,128)(2,1)} async-done(((bf16[1,1,256,256]{3,2,1,0:T(8,128)(2,1)}), bf16[1,1,2048,256]{3,2,1,0:T(8,128)(2,1)}) %all-gather.3.cloned.1.call-update) | async-done | bytes 1048592 | tf_op jit(solution)/shard_map/all_gather | solution.py:158
  196.7 38.9 %all-gather.5.cloned.1.call-done = bf16[1,1,2048,256]{3,2,1,0:T(8,128)(2,1)} async-done(((bf16[1,1,256,256]{3,2,1,0:T(8,128)(2,1)}), bf16[1,1,2048,256]{3,2,1,0:T(8,128)(2,1)}) %all-gather.5.cloned.1.call-update) | async-done | bytes 1048592 | tf_op jit(solution)/shard_map/all_gather | solution.py:159
  237.8 4.9 %fusion.28 = f32[256,1536]{1,0:T(8,128)S(1)} fusion(bf16[256,2048]{1,0:T(8,128)(2,1)} %bitcast.38, bf16[1,2048,1536]{2,1,0:T(8,128)(2,1)} %param.34), kind=kOutput, calls=%fused_computation.43 | convolution fusion | flops 1610612736 | bytes 8912896 | tf_op jit(solution)/shard_map/dot_general | solution.py:235
  244.8 8.3 %all-to-all-start.3 = ((bf16[16,16,2048]{2,1,0:T(8,128)(2,1)}), bf16[16,16,2048]{2,1,0:T(8,128)(2,1)}, u32[]{:S(2)}, u32[]{:S(2)}) async-start(bf16[16,16,2048]{2,1,0:T(8,128)(2,1)} %bitcast.134), calls=%async_computation.4 | async-start | bytes 2097152 | tf_op jit(solution)/shard_map/all_to_all | solution.py:240
  254.6 49.1 %while.32 = (s32[]{:T(128)}, f32[2,8,256]{2,1,0:T(8,128)S(1)}, f32[2,8,256]{2,1,0:T(8,128)S(1)}, f32[2,8,256,128]{3,2,1,0:T(8,128)}, s32[4,512]{1,0:T(4,128)S(1)...) while((s32[]{:T(128)}, f32[2,8,256]{2,1,0:T(8,128)S(1)}, ...), condition=%wide.region_6.7_spmd.clone, body=%wide.region_0.0_spmd.clone.sunk | while | flops 1102324992 | bytes 49558864 | solution.py:38
  256.0 11.0 %conditional.6 = ((f32[2,8,256]{2,1,0:T(8,128)S(1)}, f32[2,8,256]{2,1,0:T(8,128)S(1)}, f32[2,8,256,128]{3,2,1,0:T(8,128)})) conditional(s32[]{:T(128)} %convert_element_type.148, (f32[2,8,256]{2,1,0:T(8,128)S(1)}, f32[2,8,256]{2,1,0:T(8,128)S(1)}, f32[2,8,256,128]{3,2,1,0:T(8,128)}) %tuple.99, (pred[512]{0:T(512)(128)(4,1)S(1)}, s32[512]{0:T(512)S(1)}, ...), branch_computations={%region_2.2_spmd, %region_3.5_spmd} | conditional | flops 1102323968 | bytes 49550944 | solution.py:103
  257.3 2.7 fusion.2
  262.1 3.5 %multiply_add_fusion = f32[2,8,256,128]{3,2,1,0:T(8,128)S(1)} fusion(f32[2,8,256,128]{3,2,1,0:T(8,128)S(1)} %copy-done.1, bf16[512,2,128,1]{0,2,3,1:T(8,128)(2,1)S(1)} %bitcast.130, f32[2,512,256,8]{2,1,3,0:T(8,128)S(1)} %get-tuple-element.479, f32[2,8,256]{2,1,0:T(8,128)S(1)} %max.10, pred[256,512]{0,1:T(8,128)(4,1)S(1)} %compare_and_fusion, ...), kind=kOutput, calls=%fused_computation.11 | convolution fusion | flops 548405248 | bytes 13008896 | tf_op jit(solution)/shard_map/while/body/eval_jaxpr/cond/branch_1_fun/hgqk,khd->hgqd/dot_general | solution.py:95
  268.2 11.0 %conditional.6 = ((f32[2,8,256]{2,1,0:T(8,128)S(1)}, f32[2,8,256]{2,1,0:T(8,128)S(1)}, f32[2,8,256,128]{3,2,1,0:T(8,128)})) conditional(s32[]{:T(128)} %convert_element_type.148, (f32[2,8,256]{2,1,0:T(8,128)S(1)}, f32[2,8,256]{2,1,0:T(8,128)S(1)}, f32[2,8,256,128]{3,2,1,0:T(8,128)}) %tuple.99, (pred[512]{0:T(512)(128)(4,1)S(1)}, s32[512]{0:T(512)S(1)}, ...), branch_computations={%region_2.2_spmd, %region_3.5_spmd} | conditional | flops 1102323968 | bytes 49550944 | solution.py:103
  274.4 3.5 %multiply_add_fusion = f32[2,8,256,128]{3,2,1,0:T(8,128)S(1)} fusion(f32[2,8,256,128]{3,2,1,0:T(8,128)S(1)} %copy-done.1, bf16[512,2,128,1]{0,2,3,1:T(8,128)(2,1)S(1)} %bitcast.130, f32[2,512,256,8]{2,1,3,0:T(8,128)S(1)} %get-tuple-element.479, f32[2,8,256]{2,1,0:T(8,128)S(1)} %max.10, pred[256,512]{0,1:T(8,128)(4,1)S(1)} %compare_and_fusion, ...), kind=kOutput, calls=%fused_computation.11 | convolution fusion | flops 548405248 | bytes 13008896 | tf_op jit(solution)/shard_map/while/body/eval_jaxpr/cond/branch_1_fun/hgqk,khd->hgqd/dot_general | solution.py:95
  280.5 11.0 %conditional.6 = ((f32[2,8,256]{2,1,0:T(8,128)S(1)}, f32[2,8,256]{2,1,0:T(8,128)S(1)}, f32[2,8,256,128]{3,2,1,0:T(8,128)})) conditional(s32[]{:T(128)} %convert_element_type.148, (f32[2,8,256]{2,1,0:T(8,128)S(1)}, f32[2,8,256]{2,1,0:T(8,128)S(1)}, f32[2,8,256,128]{3,2,1,0:T(8,128)}) %tuple.99, (pred[512]{0:T(512)(128)(4,1)S(1)}, s32[512]{0:T(512)S(1)}, ...), branch_computations={%region_2.2_spmd, %region_3.5_spmd} | conditional | flops 1102323968 | bytes 49550944 | solution.py:103
  286.6 3.5 %multiply_add_fusion = f32[2,8,256,128]{3,2,1,0:T(8,128)S(1)} fusion(f32[2,8,256,128]{3,2,1,0:T(8,128)S(1)} %copy-done.1, bf16[512,2,128,1]{0,2,3,1:T(8,128)(2,1)S(1)} %bitcast.130, f32[2,512,256,8]{2,1,3,0:T(8,128)S(1)} %get-tuple-element.479, f32[2,8,256]{2,1,0:T(8,128)S(1)} %max.10, pred[256,512]{0,1:T(8,128)(4,1)S(1)} %compare_and_fusion, ...), kind=kOutput, calls=%fused_computation.11 | convolution fusion | flops 548405248 | bytes 13008896 | tf_op jit(solution)/shard_map/while/body/eval_jaxpr/cond/branch_1_fun/hgqk,khd->hgqd/dot_general | solution.py:95
  292.8 11.0 %conditional.6 = ((f32[2,8,256]{2,1,0:T(8,128)S(1)}, f32[2,8,256]{2,1,0:T(8,128)S(1)}, f32[2,8,256,128]{3,2,1,0:T(8,128)})) conditional(s32[]{:T(128)} %convert_element_type.148, (f32[2,8,256]{2,1,0:T(8,128)S(1)}, f32[2,8,256]{2,1,0:T(8,128)S(1)}, f32[2,8,256,128]{3,2,1,0:T(8,128)}) %tuple.99, (pred[512]{0:T(512)(128)(4,1)S(1)}, s32[512]{0:T(512)S(1)}, ...), branch_computations={%region_2.2_spmd, %region_3.5_spmd} | conditional | flops 1102323968 | bytes 49550944 | solution.py:103
  298.9 3.5 %multiply_add_fusion = f32[2,8,256,128]{3,2,1,0:T(8,128)S(1)} fusion(f32[2,8,256,128]{3,2,1,0:T(8,128)S(1)} %copy-done.1, bf16[512,2,128,1]{0,2,3,1:T(8,128)(2,1)S(1)} %bitcast.130, f32[2,512,256,8]{2,1,3,0:T(8,128)S(1)} %get-tuple-element.479, f32[2,8,256]{2,1,0:T(8,128)S(1)} %max.10, pred[256,512]{0,1:T(8,128)(4,1)S(1)} %compare_and_fusion, ...), kind=kOutput, calls=%fused_computation.11 | convolution fusion | flops 548405248 | bytes 13008896 | tf_op jit(solution)/shard_map/while/body/eval_jaxpr/cond/branch_1_fun/hgqk,khd->hgqd/dot_general | solution.py:95
  312.1 3.6 %gather_fusion = bf16[128,2048]{1,0:T(8,128)(2,1)} fusion(bf16[256,2048]{1,0:T(8,128)(2,1)} %bitcast.42, s32[1024]{0:T(1024)S(1)} %pad_clamp_fusion), kind=kCustom, calls=%fused_computation.2 | custom fusion | bytes 1049088 | tf_op jit(solution)/shard_map/gather | solution.py:241
  (181 shorter events, 96.9 us)
Async XLA Ops:
  7.2 235.6 %copy-start = (bf16[1,768,2048]{2,1,0:T(8,128)(2,1)S(1)}, bf16[1,768,2048]{2,1,0:T(8,128)(2,1)}, u32[]{:S(2)}) copy-start(bf16[1,768,2048]{2,1,0:T(8,128)(2,1)} %param.35) | copy-start | bytes 9437188
  7.2 38.4 %copy-start.5 = (bf16[1,1,128,256]{3,2,1,0:T(8,128)(2,1)S(1)}, bf16[1,1,128,256]{3,2,1,0:T(8,128)(2,1)}, u32[]{:S(2)}) copy-start(bf16[1,1,128,256]{3,2,1,0:T(8,128)(2,1)} %param.28) | copy-start | bytes 196612
  7.2 38.8 %copy-start.10 = (bf16[1,1,128,256]{3,2,1,0:T(8,128)(2,1)S(1)}, bf16[1,1,128,256]{3,2,1,0:T(8,128)(2,1)}, u32[]{:S(2)}) copy-start(bf16[1,1,128,256]{3,2,1,0:T(8,128)(2,1)} %param.30) | copy-start | bytes 196612
  7.2 40.4 %copy-start.12 = (s32[2,1]{0,1:T(1,128)S(1)}, s32[2,1]{0,1:T(1,128)}, u32[]{:S(2)}) copy-start(s32[2,1]{0,1:T(1,128)} %param.27) | copy-start | bytes 28
  9.0 4.6 %collective-permute-start.1 = (bf16[1,1,256,256]{2,3,1,0:T(8,128)(2,1)}, bf16[1,1,256,256]{2,3,1,0:T(8,128)(2,1)S(1)}, u32[]{:S(2)}, u32[]{:S(2)}) collective-permute-start(bf16[1,1,256,256]{2,3,1,0:T(8,128)(2,1)} %copy.74), channel_id=1, source_target_pairs={{0,16},{16,0},{1,17},{17,1},{2,18},{18,2},{3,19},{19,3},{4,20},{20... | collective-permute-start | bytes 393224 | tf_op jit(solution)/shard_map/ppermute | solution.py:21
  11.9 4.0 %collective-permute-start = (bf16[1,1,256,256]{2,3,1,0:T(8,128)(2,1)}, bf16[1,1,256,256]{2,3,1,0:T(8,128)(2,1)S(1)}, u32[]{:S(2)}, u32[]{:S(2)}) collective-permute-start(bf16[1,1,256,256]{2,3,1,0:T(8,128)(2,1)} %copy.71), channel_id=1, source_target_pairs={{0,16},{16,0},{1,17},{17,1},{2,18},{18,2},{3,19},{19,3},{4,20},{20... | collective-permute-start | bytes 393224 | tf_op jit(solution)/shard_map/ppermute | solution.py:21
  39.3 17.9 %all-to-all-start.1 = ((bf16[256,8,128]{2,0,1:T(8,128)(2,1)}), bf16[256,8,128]{2,0,1:T(8,128)(2,1)}, u32[]{:S(2)}, u32[]{:S(2)}) async-start(bf16[256,8,128]{2,0,1:T(8,128)(2,1)} %get-tuple-element.485), calls=%async_computation.1 | async-start | bytes 1048576 | tf_op jit(solution)/shard_map/all_to_all | solution.py:156
  45.6 97.2 %reduce-scatter.2.cloned.1.call-start = ((), (), s32[]{:S(2)}) async-start(), calls=%async_computation.7 | async-start | bytes 589824 | tf_op jit(solution)/shard_map/reduce_scatter | solution.py:202
  57.2 22.1 %copy-start.8 = (s32[1,1,16,8]{2,3,1,0:T(8,128)S(1)}, s32[1,1,16,8]{2,3,1,0:T(8,128)}, u32[]{:S(2)}) copy-start(s32[1,1,16,8]{2,3,1,0:T(8,128)} %param.36) | copy-start | bytes 1540
  57.3 85.5 %copy-start.3 = (bf16[1,1,16,2048]{3,2,1,0:T(8,128)(2,1)S(1)}, bf16[1,1,16,2048]{3,2,1,0:T(8,128)(2,1)}, u32[]{:S(2)}) copy-start(bf16[1,1,16,2048]{3,2,1,0:T(8,128)(2,1)} %param.31) | copy-start | bytes 196612
  74.5 85.0 %copy-start.11 = (f32[1,1,16,8]{2,3,1,0:T(8,128)S(1)}, f32[1,1,16,8]{2,3,1,0:T(8,128)}, u32[]{:S(2)}) copy-start(f32[1,1,16,8]{2,3,1,0:T(8,128)} %param.37) | copy-start | bytes 1540
  78.6 115.8 %all-gather.3.cloned.1.call-start = ((), (), s32[]{:S(2)}) async-start(), calls=%async_computation.5 | async-start | bytes 1179648 | tf_op jit(solution)/shard_map/all_gather | solution.py:158
  146.1 91.7 %all-to-all-start.2 = ((bf16[16,16,2048]{2,1,0:T(8,128)(2,1)}), bf16[16,16,2048]{2,1,0:T(8,128)(2,1)}, u32[]{:S(2)}, u32[]{:S(2)}) async-start(bf16[16,16,2048]{2,1,0:T(8,128)(2,1)} %bitcast.131), calls=%async_computation.3 | async-start | bytes 2097152 | tf_op jit(solution)/shard_map/all_to_all | solution.py:233
  154.0 81.5 %all-gather.5.cloned.1.call-start = ((), (), s32[]{:S(2)}) async-start(), calls=%async_computation.6 | async-start | bytes 1179648 | tf_op jit(solution)/shard_map/all_gather | solution.py:159
  244.8 67.3 %all-to-all-start.3 = ((bf16[16,16,2048]{2,1,0:T(8,128)(2,1)}), bf16[16,16,2048]{2,1,0:T(8,128)(2,1)}, u32[]{:S(2)}, u32[]{:S(2)}) async-start(bf16[16,16,2048]{2,1,0:T(8,128)(2,1)} %bitcast.134), calls=%async_computation.4 | async-start | bytes 2097152 | tf_op jit(solution)/shard_map/all_to_all | solution.py:240
  260.0 2.1 copy-start.1
  265.6 1.3 copy-start.2
  272.3 2.1 copy-start.1
  277.8 1.3 copy-start.2
  284.6 2.1 copy-start.1
  290.1 1.3 copy-start.2
  296.8 2.1 copy-start.1
  302.4 1.3 copy-start.2
  305.7 11.5 %copy-start.4 = (bf16[16,2048]{1,0:T(8,128)(2,1)S(1)}, bf16[16,2048]{1,0:T(8,128)(2,1)}, u32[]{:S(2)}) copy-start(bf16[16,2048]{1,0:T(8,128)(2,1)} %reduce-scatter.2.cloned.1.call-done) | copy-start | bytes 196612
  (3 other events, 1.9 us)
Sparse Core Ops, SparseCore 0:
  78.7 64.0 reduce-scatter.1
  144.9 49.4 all-gather.2
  196.5 38.9 all-gather.4
where the time goes:
time: 326 us; the launch traced here: 324 us
  waiting for transfers between devices  146 us (45%)
  matrix products  44 us (13%)
  local copies, waits for them, and re-layouts  40.7 us (12%)
  other arithmetic  32.3 us (10%)
  starting transfers between devices  24 us (7%)
  blocking collectives  16.7 us (5%)
  between operations  14.6 us (4%)
  loops' own time  5.96 us (2%)
    reduce_scatter x1, waiting for transfers between devices, body(): lax.psum_scatter(jnp.dot(dec_attn, w_out, preferred_element_type=jnp.floa...  61.8 us
    all_gather x1, waiting for transfers between devices, body(): value_piece = lax.all_gather(prompt_values, 'ctx', axis=2, tiled=True)  38.9 us
    all_gather x1, waiting for transfers between devices, body(): key_piece = lax.all_gather(prompt_keys, 'ctx', axis=2, tiled=True)  33.7 us
    all_to_all x1, blocking collectives, body(): lax.all_to_all(key_chosen, 'ctx', split_axis=1, concat_axis=0, tiled=True)  16.7 us
    unnamed x32, local copies, waits for them, and re-layouts  14.8 us
    dot_general x4, matrix products, prefill_compute(): jnp.einsum('hgqk,khd->hgqd', weights.astype(jnp.bfloat16), value_parts, p...  13.8 us
    dot_general x4, matrix products, prefill_compute(): jnp.einsum('qhgd,khd->hgqk', query_tensor, key_parts, preferred_element_t...  10.9 us
    all_to_all x1, waiting for transfers between devices, body(): lax.all_to_all(value_chosen, 'ctx', split_axis=1, concat_axis=0, tiled=True)  8.31 us
  transfers between devices with their start and end apart: 8, of which 6 were waited for; matrix products, arithmetic and copies ran while one was open for 22% of the time, Pallas kernels for 0%

commit v1 on v0

--- a/solution.py
+++ b/solution.py
@@ -9,6 +9,21 @@
 KEY_VALUE_HEADS = 2
 NEGATIVE_LIMIT = -1e30
 EPSILON = 1e-06
+
+
+def number_columns_all(original, out_dim):
+    axis_tag = "ctx"
+    slots = lax.axis_size(axis_tag)
+    next_value = sorted(((t, (t + 1) % slots) for t in range(slots)))
+    val = original
+    gallery = [val]
+    for k0 in tuple(range(1, slots)):
+        val = lax.ppermute(val, axis_name=axis_tag, perm=next_value)
+        gallery.insert(0, val)
+    formed = jnp.concatenate(gallery, axis=out_dim)
+    parts_out = lax.axis_index(axis_tag)
+    kept_arr = parts_out + 1
+    return jnp.roll(formed, shift=kept_arr * original.shape[out_dim], axis=out_dim)
 
 
 def from_partner(block, axis, apart):
@@ -156,7 +171,7 @@
         lax.all_to_all(value_chosen, "ctx", split_axis=1, concat_axis=0, tiled=True),
     )
     key_piece = lax.all_gather(prompt_keys, "ctx", axis=2, tiled=True)
-    value_piece = lax.all_gather(prompt_values, "ctx", axis=2, tiled=True)
+    value_piece = number_columns_all(prompt_values, 2)
     row_count = key_piece.shape[2]
     positions = lax.iota(jnp.int32, row_count)
     pre_state = blockwise(

time: 326 us -> 289 us (0.89)
  waiting for transfers between devices: 146 us -> 56.1 us
  local copies, waits for them, and re-layouts: 40.7 us -> 66 us
  starting transfers between devices: 24 us -> 43.2 us
  other arithmetic: 32.3 us -> 40.4 us
    reduce_scatter x1, waiting for transfers between devices: 61.8 us -> 16.2 us  [body(): lax.psum_scatter(jnp.dot(dec_attn, w_out, preferred_element_type=jnp.floa...]
    all_gather x1 -> x0, waiting for transfers between devices: 38.9 us -> none  [body(): value_piece = lax.all_gather(prompt_values, 'ctx', axis=2, tiled=True)]
    ppermute x0 -> x7, starting transfers between devices: none -> 19.2 us  [number_columns_all(): val = lax.ppermute(val, axis_name=axis_tag, perm=next_value)]
    unnamed x32 -> x55, local copies, waits for them, and re-layouts: 14.8 us -> 32.8 us
    all_gather x1, waiting for transfers between devices: 33.7 us -> 17 us  [body(): key_piece = lax.all_gather(prompt_keys, 'ctx', axis=2, tiled=True)]
    ppermute x0 -> x7, waiting for transfers between devices: none -> 10.2 us  [number_columns_all(): val = lax.ppermute(val, axis_name=axis_tag, perm=next_value)]
    add x3, other arithmetic: 0.05 us -> 3.77 us  [decode_compute(): run_sum = rescale * run_sum + weights.sum(-1)]
  transfers between devices with their start and end apart: 8 -> 14, of which waited for: 6 -> 10; matrix products, arithmetic and copies ran while one was open for 22% -> 36% of each run, Pallas kernels for 0% -> 0%
where the time goes in v1:
time: 289 us; the launch traced here: 287 us
  local copies, waits for them, and re-layouts  66 us (23%)
  waiting for transfers between devices  56.1 us (19%)
  matrix products  43.9 us (15%)
  starting transfers between devices  43.2 us (15%)
  other arithmetic  40.4 us (14%)
  blocking collectives  16.7 us (6%)
  between operations  15 us (5%)
  loops' own time  5.74 us (2%)
    unnamed x55, local copies, waits for them, and re-layouts  32.8 us
    ppermute x7, starting transfers between devices, number_columns_all(): val = lax.ppermute(val, axis_name=axis_tag, perm=next_value)  19.2 us
    all_gather x1, waiting for transfers between devices, body(): key_piece = lax.all_gather(prompt_keys, 'ctx', axis=2, tiled=True)  17 us
    all_to_all x1, blocking collectives, body(): lax.all_to_all(key_chosen, 'ctx', split_axis=1, concat_axis=0, tiled=True)  16.7 us
    reduce_scatter x1, waiting for transfers between devices, body(): lax.psum_scatter(jnp.dot(dec_attn, w_out, preferred_element_type=jnp.floa...  16.2 us
    dot_general x4, matrix products, prefill_compute(): jnp.einsum('hgqk,khd->hgqd', weights.astype(jnp.bfloat16), value_parts, p...  13.8 us
    dot_general x4, matrix products, prefill_compute(): jnp.einsum('qhgd,khd->hgqk', query_tensor, key_parts, preferred_element_t...  10.9 us
    ppermute x7, waiting for transfers between devices, number_columns_all(): val = lax.ppermute(val, axis_name=axis_tag, perm=next_value)  10.2 us
  transfers between devices with their start and end apart: 14, of which 10 were waited for; matrix products, arithmetic and copies ran while one was open for 36% of the time, Pallas kernels for 0%

profile of v1, /device:TPU:25, one launch (start us, length us, event | category | flops | bytes accessed | tf_op | source)
XLA Modules:
  0.0 287.1 jit_solution(11985209274923861438)
XLA Ops:
  20.5 16.7 %all_to_all.40 = bf16[256,8,128]{2,0,1:T(8,128)(2,1)} all-to-all(bf16[256,8,128]{2,0,1:T(8,128)(2,1)S(1)} %get-tuple-element.486), channel_id=1, replica_groups=mesh['group'=2,'ctx'=8,'exp'=2] {'ctx'}, dimensions={1} | all-to-all | bytes 1048576 | tf_op jit(solution)/shard_map/all_to_all | solution.py:170
  37.2 6.3 %all-to-all-start.1 = ((bf16[256,8,128]{2,0,1:T(8,128)(2,1)}), bf16[256,8,128]{2,0,1:T(8,128)(2,1)}, u32[]{:S(2)}, u32[]{:S(2)}) async-start(bf16[256,8,128]{2,0,1:T(8,128)(2,1)} %get-tuple-element.485), calls=%async_computation.1 | async-start | bytes 1048576 | tf_op jit(solution)/shard_map/all_to_all | solution.py:171
  46.0 9.1 %all-to-all-done.1 = bf16[256,8,128]{2,0,1:T(8,128)(2,1)} async-done(((bf16[256,8,128]{2,0,1:T(8,128)(2,1)}), bf16[256,8,128]{2,0,1:T(8,128)(2,1)}, u32[]{:S(2)}, u32[]{:S(2)}) %all-to-all-start.1) | async-done | bytes 524320 | tf_op jit(solution)/shard_map/all_to_all | solution.py:171
  55.7 19.5 %while.31 = (s32[]{:T(128)}, f32[2,128]{1,0:T(2,128)S(1)}, f32[2,128]{1,0:T(2,128)}, f32[2,128,128]{2,1,0:T(8,128)S(1)}, s32[4,512]{1,0:T(4,128)S(1)}, /*index=5...) while((s32[]{:T(128)}, f32[2,128]{1,0:T(2,128)S(1)}, ...), condition=%wide.region_13.15_spmd, body=%wide.region_7.14_spmd.sunk | while | flops 68355584 | bytes 2185460 | solution.py:53
  57.6 4.0 %conditional.5 = ((f32[2,128]{1,0:T(2,128)S(1)}, f32[2,128]{1,0:T(2,128)}, f32[2,128,128]{2,1,0:T(8,128)S(1)})) conditional(s32[]{:T(128)} %convert_element_type.147, (f32[2,128]{1,0:T(2,128)S(1)}, f32[2,128]{1,0:T(2,128)}, f32[2,128,128]{2,1,0:T(8,128)S(1)}) %tuple.95, (pred[1,512]{1,0:T(4,128)(4,1)S(1)}, bf16[4,512,128]{2,1,0:T(8,128)(2,1)}, ...), branch_computations={%region_9.10_spmd, %region_10.13_spmd} | conditional | flops 68354560 | bytes 2182689 | solution.py:146
  63.5 4.0 %conditional.5 = ((f32[2,128]{1,0:T(2,128)S(1)}, f32[2,128]{1,0:T(2,128)}, f32[2,128,128]{2,1,0:T(8,128)S(1)})) conditional(s32[]{:T(128)} %convert_element_type.147, (f32[2,128]{1,0:T(2,128)S(1)}, f32[2,128]{1,0:T(2,128)}, f32[2,128,128]{2,1,0:T(8,128)S(1)}) %tuple.95, (pred[1,512]{1,0:T(4,128)(4,1)S(1)}, bf16[4,512,128]{2,1,0:T(8,128)(2,1)}, ...), branch_computations={%region_9.10_spmd, %region_10.13_spmd} | conditional | flops 68354560 | bytes 2182689 | solution.py:146
  69.3 4.0 %conditional.5 = ((f32[2,128]{1,0:T(2,128)S(1)}, f32[2,128]{1,0:T(2,128)}, f32[2,128,128]{2,1,0:T(8,128)S(1)})) conditional(s32[]{:T(128)} %convert_element_type.147, (f32[2,128]{1,0:T(2,128)S(1)}, f32[2,128]{1,0:T(2,128)}, f32[2,128,128]{2,1,0:T(8,128)S(1)}) %tuple.95, (pred[1,512]{1,0:T(4,128)(4,1)S(1)}, bf16[4,512,128]{2,1,0:T(8,128)(2,1)}, ...), branch_computations={%region_9.10_spmd, %region_10.13_spmd} | conditional | flops 68354560 | bytes 2182689 | solution.py:146
  98.7 4.9 %collective-permute-start.3 = (bf16[1,1,256,256]{3,2,1,0:T(8,128)(2,1)}, bf16[1,1,256,256]{3,2,1,0:T(8,128)(2,1)}, u32[]{:S(2)}, u32[]{:S(2)}) collective-permute-start(bf16[1,1,256,256]{3,2,1,0:T(8,128)(2,1)} %collective-permute-done.2), channel_id=1, source_target_pairs={{0,2},{2,4},{4,6},{6,8},{8,10},{10,12},{12,14},{14,0},{1,3},{3,5},... | collective-permute-start | bytes 393224 | tf_op jit(solution)/shard_map/ppermute | solution.py:21
  117.5 3.8 %collective-permute-start.6 = (bf16[1,1,256,256]{3,2,1,0:T(8,128)(2,1)}, bf16[1,1,256,256]{3,2,1,0:T(8,128)(2,1)}, u32[]{:S(2)}, u32[]{:S(2)}) collective-permute-start(bf16[1,1,256,256]{3,2,1,0:T(8,128)(2,1)} %collective-permute-done.5), channel_id=1, source_target_pairs={{0,2},{2,4},{4,6},{6,8},{8,10},{10,12},{12,14},{14,0},{1,3},{3,5},... | collective-permute-start | bytes 393224 | tf_op jit(solution)/shard_map/ppermute | solution.py:21
  130.2 16.2 %reduce-scatter.2.cloned.1.call-done = bf16[16,2048]{1,0:T(8,128)(2,1)} async-done(((bf16[128,2048]{1,0:T(8,128)(2,1)}), bf16[16,2048]{1,0:T(8,128)(2,1)}) %reduce-scatter.2.cloned.1.call-update) | async-done | bytes 65552 | tf_op jit(solution)/shard_map/reduce_scatter | solution.py:217
  149.8 7.9 %all-to-all-start.2 = ((bf16[16,16,2048]{2,1,0:T(8,128)(2,1)}), bf16[16,16,2048]{2,1,0:T(8,128)(2,1)}, u32[]{:S(2)}, u32[]{:S(2)}) async-start(bf16[16,16,2048]{2,1,0:T(8,128)(2,1)} %bitcast.132), calls=%async_computation.3 | async-start | bytes 2097152 | tf_op jit(solution)/shard_map/all_to_all | solution.py:248
  181.2 17.0 %all-gather.2.cloned.1.call-done = bf16[1,1,2048,256]{3,2,1,0:T(8,128)(2,1)} async-done(((bf16[1,1,256,256]{3,2,1,0:T(8,128)(2,1)}), bf16[1,1,2048,256]{3,2,1,0:T(8,128)(2,1)}) %all-gather.2.cloned.1.call-update) | async-done | bytes 1048592 | tf_op jit(solution)/shard_map/all_gather | solution.py:173
  200.4 4.9 %fusion.28 = f32[256,1536]{1,0:T(8,128)S(1)} fusion(bf16[256,2048]{1,0:T(8,128)(2,1)} %bitcast.38, bf16[1,2048,1536]{2,1,0:T(8,128)(2,1)} %param.34), kind=kOutput, calls=%fused_computation.43 | convolution fusion | flops 1610612736 | bytes 8912896 | tf_op jit(solution)/shard_map/dot_general | solution.py:250
  207.4 8.3 %all-to-all-start.3 = ((bf16[16,16,2048]{2,1,0:T(8,128)(2,1)}), bf16[16,16,2048]{2,1,0:T(8,128)(2,1)}, u32[]{:S(2)}, u32[]{:S(2)}) async-start(bf16[16,16,2048]{2,1,0:T(8,128)(2,1)} %bitcast.136), calls=%async_computation.4 | async-start | bytes 2097152 | tf_op jit(solution)/shard_map/all_to_all | solution.py:255
  217.2 48.9 %while.32 = (s32[]{:T(128)}, f32[2,8,256]{2,1,0:T(8,128)S(1)}, f32[2,8,256]{2,1,0:T(8,128)S(1)}, f32[2,8,256,128]{3,2,1,0:T(8,128)}, s32[4,512]{1,0:T(4,128)S(1)...) while((s32[]{:T(128)}, f32[2,8,256]{2,1,0:T(8,128)S(1)}, ...), condition=%wide.region_6.7_spmd.clone, body=%wide.region_0.0_spmd.clone.sunk | while | flops 1102324992 | bytes 49558864 | solution.py:53
  218.5 10.9 %conditional.6 = ((f32[2,8,256]{2,1,0:T(8,128)S(1)}, f32[2,8,256]{2,1,0:T(8,128)S(1)}, f32[2,8,256,128]{3,2,1,0:T(8,128)})) conditional(s32[]{:T(128)} %convert_element_type.148, (f32[2,8,256]{2,1,0:T(8,128)S(1)}, f32[2,8,256]{2,1,0:T(8,128)S(1)}, f32[2,8,256,128]{3,2,1,0:T(8,128)}) %tuple.99, (pred[512]{0:T(512)(128)(4,1)S(1)}, s32[512]{0:T(512)S(1)}, ...), branch_computations={%region_2.2_spmd, %region_3.5_spmd} | conditional | flops 1102323968 | bytes 49550944 | solution.py:118
  224.6 3.5 %multiply_add_fusion = f32[2,8,256,128]{3,2,1,0:T(8,128)S(1)} fusion(f32[2,8,256,128]{3,2,1,0:T(8,128)S(1)} %copy-done.1, bf16[512,2,128,1]{0,2,3,1:T(8,128)(2,1)S(1)} %bitcast.130, f32[2,512,256,8]{2,1,3,0:T(8,128)S(1)} %get-tuple-element.479, f32[2,8,256]{2,1,0:T(8,128)S(1)} %max.10, pred[256,512]{0,1:T(8,128)(4,1)S(1)} %compare_and_fusion, ...), kind=kOutput, calls=%fused_computation.11 | convolution fusion | flops 548405248 | bytes 13008896 | tf_op jit(solution)/shard_map/while/body/eval_jaxpr/cond/branch_1_fun/hgqk,khd->hgqd/dot_general | solution.py:110
  230.7 10.9 %conditional.6 = ((f32[2,8,256]{2,1,0:T(8,128)S(1)}, f32[2,8,256]{2,1,0:T(8,128)S(1)}, f32[2,8,256,128]{3,2,1,0:T(8,128)})) conditional(s32[]{:T(128)} %convert_element_type.148, (f32[2,8,256]{2,1,0:T(8,128)S(1)}, f32[2,8,256]{2,1,0:T(8,128)S(1)}, f32[2,8,256,128]{3,2,1,0:T(8,128)}) %tuple.99, (pred[512]{0:T(512)(128)(4,1)S(1)}, s32[512]{0:T(512)S(1)}, ...), branch_computations={%region_2.2_spmd, %region_3.5_spmd} | conditional | flops 1102323968 | bytes 49550944 | solution.py:118
  236.9 3.5 %multiply_add_fusion = f32[2,8,256,128]{3,2,1,0:T(8,128)S(1)} fusion(f32[2,8,256,128]{3,2,1,0:T(8,128)S(1)} %copy-done.1, bf16[512,2,128,1]{0,2,3,1:T(8,128)(2,1)S(1)} %bitcast.130, f32[2,512,256,8]{2,1,3,0:T(8,128)S(1)} %get-tuple-element.479, f32[2,8,256]{2,1,0:T(8,128)S(1)} %max.10, pred[256,512]{0,1:T(8,128)(4,1)S(1)} %compare_and_fusion, ...), kind=kOutput, calls=%fused_computation.11 | convolution fusion | flops 548405248 | bytes 13008896 | tf_op jit(solution)/shard_map/while/body/eval_jaxpr/cond/branch_1_fun/hgqk,khd->hgqd/dot_general | solution.py:110
  243.0 10.9 %conditional.6 = ((f32[2,8,256]{2,1,0:T(8,128)S(1)}, f32[2,8,256]{2,1,0:T(8,128)S(1)}, f32[2,8,256,128]{3,2,1,0:T(8,128)})) conditional(s32[]{:T(128)} %convert_element_type.148, (f32[2,8,256]{2,1,0:T(8,128)S(1)}, f32[2,8,256]{2,1,0:T(8,128)S(1)}, f32[2,8,256,128]{3,2,1,0:T(8,128)}) %tuple.99, (pred[512]{0:T(512)(128)(4,1)S(1)}, s32[512]{0:T(512)S(1)}, ...), branch_computations={%region_2.2_spmd, %region_3.5_spmd} | conditional | flops 1102323968 | bytes 49550944 | solution.py:118
  249.1 3.5 %multiply_add_fusion = f32[2,8,256,128]{3,2,1,0:T(8,128)S(1)} fusion(f32[2,8,256,128]{3,2,1,0:T(8,128)S(1)} %copy-done.1, bf16[512,2,128,1]{0,2,3,1:T(8,128)(2,1)S(1)} %bitcast.130, f32[2,512,256,8]{2,1,3,0:T(8,128)S(1)} %get-tuple-element.479, f32[2,8,256]{2,1,0:T(8,128)S(1)} %max.10, pred[256,512]{0,1:T(8,128)(4,1)S(1)} %compare_and_fusion, ...), kind=kOutput, calls=%fused_computation.11 | convolution fusion | flops 548405248 | bytes 13008896 | tf_op jit(solution)/shard_map/while/body/eval_jaxpr/cond/branch_1_fun/hgqk,khd->hgqd/dot_general | solution.py:110
  255.2 10.9 %conditional.6 = ((f32[2,8,256]{2,1,0:T(8,128)S(1)}, f32[2,8,256]{2,1,0:T(8,128)S(1)}, f32[2,8,256,128]{3,2,1,0:T(8,128)})) conditional(s32[]{:T(128)} %convert_element_type.148, (f32[2,8,256]{2,1,0:T(8,128)S(1)}, f32[2,8,256]{2,1,0:T(8,128)S(1)}, f32[2,8,256,128]{3,2,1,0:T(8,128)}) %tuple.99, (pred[512]{0:T(512)(128)(4,1)S(1)}, s32[512]{0:T(512)S(1)}, ...), branch_computations={%region_2.2_spmd, %region_3.5_spmd} | conditional | flops 1102323968 | bytes 49550944 | solution.py:118
  261.3 3.5 %multiply_add_fusion = f32[2,8,256,128]{3,2,1,0:T(8,128)S(1)} fusion(f32[2,8,256,128]{3,2,1,0:T(8,128)S(1)} %copy-done.1, bf16[512,2,128,1]{0,2,3,1:T(8,128)(2,1)S(1)} %bitcast.130, f32[2,512,256,8]{2,1,3,0:T(8,128)S(1)} %get-tuple-element.479, f32[2,8,256]{2,1,0:T(8,128)S(1)} %max.10, pred[256,512]{0,1:T(8,128)(4,1)S(1)} %compare_and_fusion, ...), kind=kOutput, calls=%fused_computation.11 | convolution fusion | flops 548405248 | bytes 13008896 | tf_op jit(solution)/shard_map/while/body/eval_jaxpr/cond/branch_1_fun/hgqk,khd->hgqd/dot_general | solution.py:110
  274.5 3.6 %gather_fusion = bf16[128,2048]{1,0:T(8,128)(2,1)} fusion(bf16[256,2048]{1,0:T(8,128)(2,1)} %bitcast.42, s32[1024]{0:T(1024)S(1)} %pad_clamp_fusion), kind=kCustom, calls=%fused_computation.2 | custom fusion | bytes 1049088 | tf_op jit(solution)/shard_map/gather | solution.py:256
  (217 shorter events, 153.8 us)
Async XLA Ops:
  7.2 198.2 %copy-start = (bf16[1,768,2048]{2,1,0:T(8,128)(2,1)S(1)}, bf16[1,768,2048]{2,1,0:T(8,128)(2,1)}, u32[]{:S(2)}) copy-start(bf16[1,768,2048]{2,1,0:T(8,128)(2,1)} %param.35) | copy-start | bytes 9437188
  8.3 4.4 %collective-permute-start.8 = (bf16[1,1,256,256]{2,3,1,0:T(8,128)(2,1)S(1)}, bf16[1,1,256,256]{2,3,1,0:T(8,128)(2,1)S(1)}, u32[]{:S(2)}, u32[]{:S(2)}) collective-permute-start(bf16[1,1,256,256]{2,3,1,0:T(8,128)(2,1)S(1)} %copy.74), channel_id=1, source_target_pairs={{0,16},{16,0},{1,17},{17,1},{2,18},{18,2},{3,19},{19,3},{4,20},{20... | collective-permute-start | bytes 393224 | tf_op jit(solution)/shard_map/ppermute | solution.py:36
  11.3 4.0 %collective-permute-start.7 = (bf16[1,1,256,256]{2,3,1,0:T(8,128)(2,1)}, bf16[1,1,256,256]{2,3,1,0:T(8,128)(2,1)S(1)}, u32[]{:S(2)}, u32[]{:S(2)}) collective-permute-start(bf16[1,1,256,256]{2,3,1,0:T(8,128)(2,1)} %copy.71), channel_id=1, source_target_pairs={{0,16},{16,0},{1,17},{17,1},{2,18},{18,2},{3,19},{19,3},{4,20},{20... | collective-permute-start | bytes 393224 | tf_op jit(solution)/shard_map/ppermute | solution.py:36
  18.2 25.3 %copy-start.8 = (bf16[1,1,128,256]{3,2,1,0:T(8,128)(2,1)S(1)}, bf16[1,1,128,256]{3,2,1,0:T(8,128)(2,1)}, u32[]{:S(2)}) copy-start(bf16[1,1,128,256]{3,2,1,0:T(8,128)(2,1)} %param.28) | copy-start | bytes 196612
  18.2 25.7 %copy-start.11 = (bf16[1,1,128,256]{3,2,1,0:T(8,128)(2,1)S(1)}, bf16[1,1,128,256]{3,2,1,0:T(8,128)(2,1)}, u32[]{:S(2)}) copy-start(bf16[1,1,128,256]{3,2,1,0:T(8,128)(2,1)} %param.30) | copy-start | bytes 196612
  18.2 25.7 %copy-start.12 = (bf16[1,1,128,256]{3,2,1,0:T(8,128)(2,1)S(1)}, bf16[1,1,128,256]{3,2,1,0:T(8,128)(2,1)}, u32[]{:S(2)}) copy-start(bf16[1,1,128,256]{3,2,1,0:T(8,128)(2,1)} %param.29) | copy-start | bytes 196612
  18.2 26.5 %copy-start.15 = (s32[2,1]{0,1:T(1,128)S(1)}, s32[2,1]{0,1:T(1,128)}, u32[]{:S(2)}) copy-start(s32[2,1]{0,1:T(1,128)} %param.27) | copy-start | bytes 28
  37.2 17.9 %all-to-all-start.1 = ((bf16[256,8,128]{2,0,1:T(8,128)(2,1)}), bf16[256,8,128]{2,0,1:T(8,128)(2,1)}, u32[]{:S(2)}, u32[]{:S(2)}) async-start(bf16[256,8,128]{2,0,1:T(8,128)(2,1)} %get-tuple-element.485), calls=%async_computation.1 | async-start | bytes 1048576 | tf_op jit(solution)/shard_map/all_to_all | solution.py:171
  43.5 103.0 %reduce-scatter.2.cloned.1.call-start = ((), (), s32[]{:S(2)}) async-start(), calls=%async_computation.6 | async-start | bytes 589824 | tf_op jit(solution)/shard_map/reduce_scatter | solution.py:217
  75.2 9.7 %copy-start.9 = (s32[1,1,16,8]{2,3,1,0:T(8,128)S(1)}, s32[1,1,16,8]{2,3,1,0:T(8,128)}, u32[]{:S(2)}) copy-start(s32[1,1,16,8]{2,3,1,0:T(8,128)} %param.36) | copy-start | bytes 1540
  79.3 118.8 %all-gather.2.cloned.1.call-start = ((), (), s32[]{:S(2)}) async-start(), calls=%async_computation.5 | async-start | bytes 1179648 | tf_op jit(solution)/shard_map/all_gather | solution.py:173
  79.4 4.8 %collective-permute-start = (bf16[1,1,256,256]{3,2,1,0:T(8,128)(2,1)S(1)}, bf16[1,1,256,256]{3,2,1,0:T(8,128)(2,1)S(1)}, u32[]{:S(2)}, u32[]{:S(2)}) collective-permute-start(bf16[1,1,256,256]{3,2,1,0:T(8,128)(2,1)S(1)} %copy-done.3), channel_id=1, source_target_pairs={{0,2},{2,4},{4,6},{6,8},{8,10},{10,12},{12,14},{14,0},{1,3},{3,5},... | collective-permute-start | bytes 393224 | tf_op jit(solution)/shard_map/ppermute | solution.py:21
  84.1 5.1 %collective-permute-start.1 = (bf16[1,1,256,256]{3,2,1,0:T(8,128)(2,1)S(1)}, bf16[1,1,256,256]{3,2,1,0:T(8,128)(2,1)S(1)}, u32[]{:S(2)}, u32[]{:S(2)}) collective-permute-start(bf16[1,1,256,256]{3,2,1,0:T(8,128)(2,1)S(1)} %collective-permute-done), channel_id=1, source_target_pairs={{0,2},{2,4},{4,6},{6,8},{8,10},{10,12},{12,14},{14,0},{1,3},{3,5},... | collective-permute-start | bytes 393224 | tf_op jit(solution)/shard_map/ppermute | solution.py:21
  89.3 33.2 %copy-start.6 = (bf16[1,1,256,256]{3,2,1,0:T(8,128)(2,1)}, bf16[1,1,256,256]{3,2,1,0:T(8,128)(2,1)S(1)}, u32[]{:S(2)}) copy-start(bf16[1,1,256,256]{3,2,1,0:T(8,128)(2,1)S(1)} %collective-permute-done.1) | copy-start | bytes 393220
  89.3 9.4 %collective-permute-start.2 = (bf16[1,1,256,256]{3,2,1,0:T(8,128)(2,1)S(1)}, bf16[1,1,256,256]{3,2,1,0:T(8,128)(2,1)}, u32[]{:S(2)}, u32[]{:S(2)}) collective-permute-start(bf16[1,1,256,256]{3,2,1,0:T(8,128)(2,1)S(1)} %collective-permute-done.1), channel_id=1, source_target_pairs={{0,2},{2,4},{4,6},{6,8},{8,10},{10,12},{12,14},{14,0},{1,3},{3,5},... | collective-permute-start | bytes 393224 | tf_op jit(solution)/shard_map/ppermute | solution.py:21
  98.7 7.3 %collective-permute-start.3 = (bf16[1,1,256,256]{3,2,1,0:T(8,128)(2,1)}, bf16[1,1,256,256]{3,2,1,0:T(8,128)(2,1)}, u32[]{:S(2)}, u32[]{:S(2)}) collective-permute-start(bf16[1,1,256,256]{3,2,1,0:T(8,128)(2,1)} %collective-permute-done.2), channel_id=1, source_target_pairs={{0,2},{2,4},{4,6},{6,8},{8,10},{10,12},{12,14},{14,0},{1,3},{3,5},... | collective-permute-start | bytes 393224 | tf_op jit(solution)/shard_map/ppermute | solution.py:21
  106.0 5.4 %collective-permute-start.4 = (bf16[1,1,256,256]{3,2,1,0:T(8,128)(2,1)}, bf16[1,1,256,256]{3,2,1,0:T(8,128)(2,1)}, u32[]{:S(2)}, u32[]{:S(2)}) collective-permute-start(bf16[1,1,256,256]{3,2,1,0:T(8,128)(2,1)} %collective-permute-done.3), channel_id=1, source_target_pairs={{0,2},{2,4},{4,6},{6,8},{8,10},{10,12},{12,14},{14,0},{1,3},{3,5},... | collective-permute-start | bytes 393224 | tf_op jit(solution)/shard_map/ppermute | solution.py:21
  111.4 6.1 %collective-permute-start.5 = (bf16[1,1,256,256]{3,2,1,0:T(8,128)(2,1)}, bf16[1,1,256,256]{3,2,1,0:T(8,128)(2,1)}, u32[]{:S(2)}, u32[]{:S(2)}) collective-permute-start(bf16[1,1,256,256]{3,2,1,0:T(8,128)(2,1)} %collective-permute-done.4), channel_id=1, source_target_pairs={{0,2},{2,4},{4,6},{6,8},{8,10},{10,12},{12,14},{14,0},{1,3},{3,5},... | collective-permute-start | bytes 393224 | tf_op jit(solution)/shard_map/ppermute | solution.py:21
  117.5 11.2 %collective-permute-start.6 = (bf16[1,1,256,256]{3,2,1,0:T(8,128)(2,1)}, bf16[1,1,256,256]{3,2,1,0:T(8,128)(2,1)}, u32[]{:S(2)}, u32[]{:S(2)}) collective-permute-start(bf16[1,1,256,256]{3,2,1,0:T(8,128)(2,1)} %collective-permute-done.5), channel_id=1, source_target_pairs={{0,2},{2,4},{4,6},{6,8},{8,10},{10,12},{12,14},{14,0},{1,3},{3,5},... | collective-permute-start | bytes 393224 | tf_op jit(solution)/shard_map/ppermute | solution.py:21
  123.2 23.3 %copy-start.4 = (bf16[1,1,16,2048]{3,2,1,0:T(8,128)(2,1)S(1)}, bf16[1,1,16,2048]{3,2,1,0:T(8,128)(2,1)}, u32[]{:S(2)}) copy-start(bf16[1,1,16,2048]{3,2,1,0:T(8,128)(2,1)} %param.31) | copy-start | bytes 196612
  149.8 50.6 %all-to-all-start.2 = ((bf16[16,16,2048]{2,1,0:T(8,128)(2,1)}), bf16[16,16,2048]{2,1,0:T(8,128)(2,1)}, u32[]{:S(2)}, u32[]{:S(2)}) async-start(bf16[16,16,2048]{2,1,0:T(8,128)(2,1)} %bitcast.132), calls=%async_computation.3 | async-start | bytes 2097152 | tf_op jit(solution)/shard_map/all_to_all | solution.py:248
  157.7 17.0 %copy-start.7 = (bf16[1,1,256,256]{3,2,1,0:T(8,128)(2,1)S(1)}, bf16[1,1,256,256]{3,2,1,0:T(8,128)(2,1)}, u32[]{:S(2)}) copy-start(bf16[1,1,256,256]{3,2,1,0:T(8,128)(2,1)} %copy-done.6) | copy-start | bytes 393220
  207.4 67.1 %all-to-all-start.3 = ((bf16[16,16,2048]{2,1,0:T(8,128)(2,1)}), bf16[16,16,2048]{2,1,0:T(8,128)(2,1)}, u32[]{:S(2)}, u32[]{:S(2)}) async-start(bf16[16,16,2048]{2,1,0:T(8,128)(2,1)} %bitcast.136), calls=%async_computation.4 | async-start | bytes 2097152 | tf_op jit(solution)/shard_map/all_to_all | solution.py:255
  274.5 5.1 %copy-start.5 = (bf16[16,2048]{1,0:T(8,128)(2,1)S(1)}, bf16[16,2048]{1,0:T(8,128)(2,1)}, u32[]{:S(2)}) copy-start(bf16[16,2048]{1,0:T(8,128)(2,1)} %reduce-scatter.2.cloned.1.call-done) | copy-start | bytes 196612
  (13 other events, 34.7 us)
Sparse Core Ops, SparseCore 0:
  79.4 67.0 reduce-scatter.1
  148.6 49.4 all-gather.1
